TPU v7x, 32 devices: a whole 2x2x4 slice. The times are simulated.
32 devices in a mesh: dp: 8 (over y, x, core), seq: 4 (over z).
Axes of the slice: x: 2, y: 2, z: 4, core: 2. Of those that a mesh axis runs over, the one named last changes fastest.
Arguments:
- query: bfloat16 [8, 512, 512], P('dp', 'seq'), may hold values from -8 to 8
- key: bfloat16 [8, 512, 512], P('dp', 'seq'), may hold values from -8 to 8
- value: bfloat16 [8, 512, 512], P('dp', 'seq'), may hold values from -6 to 6
- out_ctx: bfloat16 [8, 512, 512], P('dp', 'seq'), may hold values from -6 to 6
- d_out: bfloat16 [8, 512, 512], P('dp', 'seq'), may hold values from -6 to 6
- score_bias: float32 [4, 4], P('seq'), may hold values from -2 to 2
- block_list: int32 [4, 4, 4], P('seq'), may hold values from 0 to 3, as said below
- block_count: int32 [4, 4], P('seq'), may hold values from 1 to 4, as said below
- hit_count: int32 [8], P('dp'), may hold values from 128 to 512, as said below
Outputs:
- d_query: bfloat16 [8, 512, 512], P('dp', 'seq')
- d_key: bfloat16 [8, 512, 512], P('dp', 'seq')
- d_value: bfloat16 [8, 512, 512], P('dp', 'seq')
- d_bias: float32 [4, 4], P('seq')
Inputs may be any that keep to these rules, and one draw needn't show every extreme that they name: Each list block_list[h, q] holds 4 different key blocks, the first being block q itself; only its first block_count[h, q] entries are used. `block_count`: some head has a list with all 4 entries used. `hit_count`: some event has all 512 hits real.
All inputs are finite; a program needn't handle non-finite values.
Results may differ from a plain program's by a relative error of at most 0.0049.
Values may be sent and summed in bfloat16 or wider, within the bound.
A program may use at most 64 MiB of HBM per device.

v0:
```python
import math
import jax
import jax.numpy as jnp
from jax import lax
from jax.sharding import PartitionSpec as P

MASKED = -1000000000.0


def head_grads(
    query_head,
    key_head,
    value_head,
    grad_head,
    delta_head,
    bias_row,
    list_rows,
    count_row,
    hit_limit,
    slot_end,
):
    nblocks = list_rows.shape[0]
    hits, head_dim = query_head.shape
    block = hits // nblocks
    scale = 1.0 / math.sqrt(head_dim)
    query_blocks = query_head.reshape(nblocks, block, head_dim)
    key_blocks = key_head.reshape(nblocks, block, head_dim)
    value_blocks = value_head.reshape(nblocks, block, head_dim)
    grad_blocks = grad_head.reshape(nblocks, block, head_dim)
    delta_blocks = delta_head.reshape(nblocks, block)
    within = jnp.arange(block, dtype=jnp.int32)
    block_ids = jnp.arange(nblocks, dtype=jnp.int32)
    row_valid = (jnp.arange(hits, dtype=jnp.int32) < hit_limit).reshape(nblocks, block)

    def slot_scores(slot_at):
        chosen = lax.dynamic_index_in_dim(list_rows, slot_at, axis=1, keepdims=False)
        key_taken = jnp.take(key_blocks, chosen, axis=0)
        matched = chosen[:, None] == block_ids[None, :]
        shift = jnp.sum(jnp.where(matched, bias_row[None, :], 0.0), axis=1)
        scores = (
            jnp.einsum("qid,qjd->qij", query_blocks, key_taken, preferred_element_type=jnp.float32)
            * scale
        )
        scores = scores + shift[:, None, None]
        key_real = chosen[:, None] * block + within[None, :] < hit_limit
        allowed = (slot_at < count_row)[:, None, None] & key_real[:, None, :]
        return (jnp.where(allowed, scores, MASKED), allowed, chosen, matched, key_taken)

    def first_pass(slot_at, state_now):
        row_top, row_total = state_now
        scores = slot_scores(slot_at)[0]
        new_top = jnp.maximum(row_top, jnp.max(scores, axis=2))
        row_total = row_total * jnp.exp(row_top - new_top) + jnp.sum(
            jnp.exp(scores - new_top[:, :, None]), axis=2
        )
        return (new_top, row_total)

    start_top = jnp.full((nblocks, block), -1e30, jnp.float32)
    start_total = jnp.zeros((nblocks, block), jnp.float32)
    row_top, row_total = lax.fori_loop(0, slot_end, first_pass, (start_top, start_total))
    lse = row_top + jnp.log(row_total)

    def second_pass(slot_at, state_now):
        grad_query, grad_key, grad_value, grad_bias = state_now
        scores, allowed, chosen, matched, key_taken = slot_scores(slot_at)
        value_taken = jnp.take(value_blocks, chosen, axis=0)
        probs = jnp.where(allowed & row_valid[:, :, None], jnp.exp(scores - lse[:, :, None]), 0.0)
        dprobs = jnp.einsum(
            "qid,qjd->qij", grad_blocks, value_taken, preferred_element_type=jnp.float32
        )
        dscores = probs * (dprobs - delta_blocks[:, :, None])
        probs_half = probs.astype(jnp.bfloat16)
        dscores_half = dscores.astype(jnp.bfloat16)
        grad_query = grad_query + jnp.einsum(
            "qij,qjd->qid", dscores_half, key_taken, preferred_element_type=jnp.float32
        )
        key_terms = jnp.einsum(
            "qij,qid->qjd", dscores_half, query_blocks, preferred_element_type=jnp.float32
        )
        value_terms = jnp.einsum(
            "qij,qid->qjd", probs_half, grad_blocks, preferred_element_type=jnp.float32
        )
        grad_key = grad_key.at[chosen].add(key_terms)
        grad_value = grad_value.at[chosen].add(value_terms)
        block_sums = jnp.sum(dscores, axis=(1, 2))
        grad_bias = grad_bias + jnp.sum(jnp.where(matched, block_sums[:, None], 0.0), axis=0)
        return (grad_query, grad_key, grad_value, grad_bias)

    zero_field = jnp.zeros((nblocks, block, head_dim), jnp.float32)
    start_state = (zero_field, zero_field, zero_field, jnp.zeros((nblocks,), jnp.float32))
    grad_query, grad_key, grad_value, grad_bias = lax.fori_loop(
        0, slot_end, second_pass, start_state
    )
    grad_query = (grad_query * scale).reshape(hits, head_dim).astype(jnp.bfloat16)
    grad_key = (grad_key * scale).reshape(hits, head_dim).astype(jnp.bfloat16)
    grad_value = grad_value.reshape(hits, head_dim).astype(jnp.bfloat16)
    return (grad_query, grad_key, grad_value, grad_bias)


def on_device(query, key, value, out_ctx, d_out, score_bias, block_list, block_count, hit_count):
    groups = lax.axis_size("seq")
    tok_rows = query.shape[1]
    width = query.shape[2]
    heads_here = score_bias.shape[0]
    heads_all = heads_here * groups
    head_dim = width // heads_all
    first_row = lax.axis_index("seq") * tok_rows
    hit_limit = hit_count[0]
    row_valid = first_row + jnp.arange(tok_rows, dtype=jnp.int32) < hit_limit
    grad_kept = jnp.where(row_valid[:, None], d_out[0], jnp.zeros((), jnp.bfloat16))

    def split_heads(field):
        return field.reshape(tok_rows, heads_all, head_dim)

    query_heads, key_heads, value_heads, out_heads, grad_heads = (
        lax.all_to_all(split_heads(query[0]), "seq", split_axis=1, concat_axis=0, tiled=True),
        lax.all_to_all(split_heads(key[0]), "seq", split_axis=1, concat_axis=0, tiled=True),
        lax.all_to_all(split_heads(value[0]), "seq", split_axis=1, concat_axis=0, tiled=True),
        lax.all_to_all(split_heads(out_ctx[0]), "seq", split_axis=1, concat_axis=0, tiled=True),
        lax.all_to_all(split_heads(grad_kept), "seq", split_axis=1, concat_axis=0, tiled=True),
    )
    delta_heads = jnp.sum(grad_heads.astype(jnp.float32) * out_heads.astype(jnp.float32), axis=2)
    count_row = block_count[0]
    grad_query, grad_key, grad_value, grad_bias = head_grads(
        query_heads[:, 0],
        key_heads[:, 0],
        value_heads[:, 0],
        grad_heads[:, 0],
        delta_heads[:, 0],
        score_bias[0],
        block_list[0],
        count_row,
        hit_limit,
        block_list.shape[2],
    )
    query_grads = [grad_query]
    key_grads = [grad_key]
    value_grads = [grad_value]
    bias_grads = [grad_bias]
    query_back, key_back, value_back = (
        lax.all_to_all(
            jnp.stack(query_grads, axis=1), "seq", split_axis=0, concat_axis=1, tiled=True
        ),
        lax.all_to_all(
            jnp.stack(key_grads, axis=1), "seq", split_axis=0, concat_axis=1, tiled=True
        ),
        lax.all_to_all(
            jnp.stack(value_grads, axis=1), "seq", split_axis=0, concat_axis=1, tiled=True
        ),
    )
    bias_total = lax.psum(jnp.stack(bias_grads, axis=0), "dp")
    return (
        query_back.reshape(1, tok_rows, width),
        key_back.reshape(1, tok_rows, width),
        value_back.reshape(1, tok_rows, width),
        bias_total,
    )


def solution(mesh):
    placed = (
        P("dp", "seq", None),
        P("dp", "seq", None),
        P("dp", "seq", None),
        P("dp", "seq", None),
        P("dp", "seq", None),
        P("seq", None),
        P("seq", None, None),
        P("seq", None),
        P("dp"),
    )
    return jax.shard_map(
        on_device,
        mesh=mesh,
        in_specs=placed,
        out_specs=(
            P("dp", "seq", None),
            P("dp", "seq", None),
            P("dp", "seq", None),
            P("seq", None),
        ),
        check_vma=False,
    )
```

profile of v0, /device:TPU:0, one launch (start us, length us, event | category | flops | bytes accessed | tf_op | source)
XLA Modules:
  0.0 120.0 jit_solution(9918450063467983925)
XLA Ops:
  0.6 1.7 %copy.95 = bf16[1,128,512]{1,2,0:T(8,128)(2,1)} copy(bf16[1,128,512]{2,1,0:T(8,128)(2,1)} %param.15) | data formatting | bytes 262144 | tf_op args[0]
  2.3 6.5 %all-to-all-start.1 = ((bf16[128,4,128]{0,2,1:T(8,128)(2,1)}), bf16[128,4,128]{0,2,1:T(8,128)(2,1)S(1)}, u32[]{:S(2)}, u32[]{:S(2)}) async-start(bf16[128,4,128]{0,2,1:T(8,128)(2,1)} %bitcast.7), calls=%async_computation.1 | async-start | bytes 262144 | tf_op jit(solution)/shard_map/all_to_all | solution.py:116
  8.8 0.8 copy.94
  9.5 5.3 %all-to-all-done.1 = bf16[128,4,128]{0,2,1:T(8,128)(2,1)S(1)} async-done(((bf16[128,4,128]{0,2,1:T(8,128)(2,1)}), bf16[128,4,128]{0,2,1:T(8,128)(2,1)S(1)}, u32[]{:S(2)}, u32[]{:S(2)}) %all-to-all-start.1) | async-done | bytes 131104 | tf_op jit(solution)/shard_map/all_to_all | solution.py:116
  14.9 3.5 %all-to-all-start = ((bf16[128,4,128]{0,2,1:T(8,128)(2,1)}), bf16[128,4,128]{0,2,1:T(8,128)(2,1)S(1)}, u32[]{:S(2)}, u32[]{:S(2)}) async-start(bf16[128,4,128]{0,2,1:T(8,128)(2,1)} %bitcast.3), calls=%async_computation | async-start | bytes 262144 | tf_op jit(solution)/shard_map/all_to_all | solution.py:117
  19.1 0.8 copy.99
  20.0 0.8 copy.101
  21.1 3.1 %all-to-all-done = bf16[128,4,128]{0,2,1:T(8,128)(2,1)S(1)} async-done(((bf16[128,4,128]{0,2,1:T(8,128)(2,1)}), bf16[128,4,128]{0,2,1:T(8,128)(2,1)S(1)}, u32[]{:S(2)}, u32[]{:S(2)}) %all-to-all-start) | async-done | bytes 131104 | tf_op jit(solution)/shard_map/all_to_all | solution.py:117
  24.2 3.3 %all-to-all-start.2 = ((bf16[128,4,128]{0,2,1:T(8,128)(2,1)}), bf16[128,4,128]{0,2,1:T(8,128)(2,1)S(1)}, u32[]{:S(2)}, u32[]{:S(2)}) async-start(bf16[128,4,128]{0,2,1:T(8,128)(2,1)} %bitcast.15), calls=%async_computation.2 | async-start | bytes 262144 | tf_op jit(solution)/shard_map/all_to_all | solution.py:118
  27.5 0.7 broadcast_select_fusion.4
  28.5 4.9 %all-to-all-done.2 = bf16[128,4,128]{0,2,1:T(8,128)(2,1)S(1)} async-done(((bf16[128,4,128]{0,2,1:T(8,128)(2,1)}), bf16[128,4,128]{0,2,1:T(8,128)(2,1)S(1)}, u32[]{:S(2)}, u32[]{:S(2)}) %all-to-all-start.2) | async-done | bytes 131104 | tf_op jit(solution)/shard_map/all_to_all | solution.py:118
  33.4 3.3 %all-to-all-start.3 = ((bf16[128,4,128]{0,2,1:T(8,128)(2,1)}), bf16[128,4,128]{0,2,1:T(8,128)(2,1)S(1)}, u32[]{:S(2)}, u32[]{:S(2)}) async-start(bf16[128,4,128]{0,2,1:T(8,128)(2,1)} %broadcast_select_fusion.4), calls=%async_computation.3 | async-start | bytes 262144 | tf_op jit(solution)/shard_map/all_to_all | solution.py:120
  36.8 0.6 copy-done.4
  37.4 7.7 %while.38 = (s32[]{:T(128)}, f32[4,128]{1,0:T(4,128)S(1)}, f32[4,128]{1,0:T(4,128)S(1)}, s32[4]{0:T(128)S(1)}, s32[4,4]{0,1:T(4,128)S(1)}, /*index=5*/s32[]{:T(1...) while((s32[]{:T(128)}, f32[4,128]{1,0:T(4,128)S(1)}, ...), condition=%wide.region_4.6_spmd.clone, body=%wide.region_0.5_spmd.clone.sunk | while | flops 17241176 | bytes 1081720 | solution.py:60
  37.5 0.7 fusion.83
  38.4 0.6 gather_fusion
  39.4 0.7 fusion.83
  40.3 0.6 gather_fusion
  41.3 0.7 fusion.83
  42.2 0.6 gather_fusion
  43.2 0.7 fusion.83
  44.1 0.6 gather_fusion
  45.2 5.1 %all-to-all-start.4 = ((bf16[128,4,128]{0,2,1:T(8,128)(2,1)}), bf16[128,4,128]{0,2,1:T(8,128)(2,1)S(1)}, u32[]{:S(2)}, u32[]{:S(2)}) async-start(bf16[128,4,128]{0,2,1:T(8,128)(2,1)} %bitcast.24), calls=%async_computation.4 | async-start | bytes 262144 | tf_op jit(solution)/shard_map/all_to_all | solution.py:119
  50.5 5.8 %all-to-all-done.4 = bf16[128,4,128]{0,2,1:T(8,128)(2,1)S(1)} async-done(((bf16[128,4,128]{0,2,1:T(8,128)(2,1)}), bf16[128,4,128]{0,2,1:T(8,128)(2,1)S(1)}, u32[]{:S(2)}, u32[]{:S(2)}) %all-to-all-start.4) | async-done | bytes 131104 | tf_op jit(solution)/shard_map/all_to_all | solution.py:119
  56.3 23.8 %while.39 = (s32[]{:T(128)}, f32[4,128,128]{2,1,0:T(8,128)S(1)}, f32[4,128,128]{2,1,0:T(8,128)S(1)}, f32[4,128,128]{2,1,0:T(8,128)S(1)}, f32[4]{0:T(128)S(1)}, /...) while((s32[]{:T(128)}, f32[4,128,128]{2,1,0:T(8,128)S(1)}, ...), condition=%wide.region_12.14_spmd.clone.clone.clone, body=%wide.region_6.0_spmd.clone.clone.clone.sunk | while | flops 85068952 | bytes 5253752 | solution.py:91
  56.4 0.7 fusion.96
  57.3 0.7 fusion.95
  58.0 0.6 gather_fusion.1
  58.6 0.6 gather_fusion.2
  60.3 0.8 scatter_fusion.1
  61.5 0.8 scatter_fusion
  62.3 0.7 fusion.96
  63.2 0.7 fusion.95
  64.0 0.6 gather_fusion.1
  64.5 0.6 gather_fusion.2
  66.3 0.8 scatter_fusion.1
  67.5 0.8 scatter_fusion
  68.3 0.7 fusion.96
  69.2 0.7 fusion.95
  69.9 0.6 gather_fusion.1
  70.5 0.6 gather_fusion.2
  72.2 0.7 scatter_fusion.1
  73.5 0.7 scatter_fusion
  74.2 0.7 fusion.96
  75.1 0.7 fusion.95
  75.9 0.6 gather_fusion.1
  76.4 0.6 gather_fusion.2
  78.2 0.7 scatter_fusion.1
  79.4 0.7 scatter_fusion
  80.7 0.7 reduce.4
  81.4 0.7 reshape.270
  82.1 3.3 %all-to-all-start.7 = ((bf16[4,2,8192]{2,1,0:T(2,128)(2,1)}), bf16[4,2,8192]{2,1,0:T(2,128)(2,1)S(1)}, u32[]{:S(2)}, u32[]{:S(2)}) async-start(bf16[4,2,8192]{2,1,0:T(2,128)(2,1)} %reshape.270), calls=%async_computation.7 | async-start | bytes 262144 | tf_op jit(solution)/shard_map/all_to_all | solution.py:147
  85.5 0.7 reduce.3
  86.2 0.7 reshape.268
  86.9 4.5 %all-to-all-done.7 = bf16[4,2,8192]{2,1,0:T(2,128)(2,1)S(1)} async-done(((bf16[4,2,8192]{2,1,0:T(2,128)(2,1)}), bf16[4,2,8192]{2,1,0:T(2,128)(2,1)S(1)}, u32[]{:S(2)}, u32[]{:S(2)}) %all-to-all-start.7) | async-done | bytes 131104 | tf_op jit(solution)/shard_map/all_to_all | solution.py:147
  91.3 3.3 %all-to-all-start.6 = ((bf16[4,2,8192]{2,1,0:T(2,128)(2,1)}), bf16[4,2,8192]{2,1,0:T(2,128)(2,1)S(1)}, u32[]{:S(2)}, u32[]{:S(2)}) async-start(bf16[4,2,8192]{2,1,0:T(2,128)(2,1)} %reshape.268), calls=%async_computation.6 | async-start | bytes 262144 | tf_op jit(solution)/shard_map/all_to_all | solution.py:144
  94.7 0.7 reduce.2
  95.3 0.7 reshape.266
  96.0 4.6 %all-to-all-done.6 = bf16[4,2,8192]{2,1,0:T(2,128)(2,1)S(1)} async-done(((bf16[4,2,8192]{2,1,0:T(2,128)(2,1)}), bf16[4,2,8192]{2,1,0:T(2,128)(2,1)S(1)}, u32[]{:S(2)}, u32[]{:S(2)}) %all-to-all-start.6) | async-done | bytes 131104 | tf_op jit(solution)/shard_map/all_to_all | solution.py:144
  100.6 3.9 %all-to-all-start.5 = ((bf16[4,2,8192]{2,1,0:T(2,128)(2,1)}), bf16[4,2,8192]{2,1,0:T(2,128)(2,1)S(1)}, u32[]{:S(2)}, u32[]{:S(2)}) async-start(bf16[4,2,8192]{2,1,0:T(2,128)(2,1)} %reshape.266), calls=%async_computation.5 | async-start | bytes 262144 | tf_op jit(solution)/shard_map/all_to_all | solution.py:141
  104.5 12.3 %psum.7 = f32[1,4]{1,0:T(1,128)} all-reduce(f32[1,4]{1,0:T(1,128)S(1)} %bitcast.144), channel_id=1, replica_groups=mesh['dp'=8,'seq'=4] {'dp'}, use_global_device_ids=true, to_apply=%region_13.15 | all-reduce | flops 4 | bytes 32 | tf_op jit(solution)/shard_map/psum | solution.py:151
  117.1 0.8 copy.115
  118.2 0.8 copy.114
  119.2 0.8 copy.113
  (138 shorter events, 12.2 us)
Async XLA Ops:
  2.3 6.5 %copy-start = (bf16[1,128,512]{2,1,0:T(8,128)(2,1)S(1)}, bf16[1,128,512]{2,1,0:T(8,128)(2,1)}, u32[]{:S(2)}) copy-start(bf16[1,128,512]{2,1,0:T(8,128)(2,1)} %param.16) | copy-start | bytes 393220
  2.3 12.6 %all-to-all-start.1 = ((bf16[128,4,128]{0,2,1:T(8,128)(2,1)}), bf16[128,4,128]{0,2,1:T(8,128)(2,1)S(1)}, u32[]{:S(2)}, u32[]{:S(2)}) async-start(bf16[128,4,128]{0,2,1:T(8,128)(2,1)} %bitcast.7), calls=%async_computation.1 | async-start | bytes 262144 | tf_op jit(solution)/shard_map/all_to_all | solution.py:116
  14.8 4.3 %copy-start.1 = (bf16[1,128,512]{2,1,0:T(8,128)(2,1)S(1)}, bf16[1,128,512]{2,1,0:T(8,128)(2,1)}, u32[]{:S(2)}) copy-start(bf16[1,128,512]{2,1,0:T(8,128)(2,1)} %param.17) | copy-start | bytes 393220
  14.9 9.4 %all-to-all-start = ((bf16[128,4,128]{0,2,1:T(8,128)(2,1)}), bf16[128,4,128]{0,2,1:T(8,128)(2,1)S(1)}, u32[]{:S(2)}, u32[]{:S(2)}) async-start(bf16[128,4,128]{0,2,1:T(8,128)(2,1)} %bitcast.3), calls=%async_computation | async-start | bytes 262144 | tf_op jit(solution)/shard_map/all_to_all | solution.py:117
  18.4 0.7 copy-start.5
  19.1 0.9 copy-start.2
  20.0 0.9 copy-start.3
  24.2 9.2 %all-to-all-start.2 = ((bf16[128,4,128]{0,2,1:T(8,128)(2,1)}), bf16[128,4,128]{0,2,1:T(8,128)(2,1)S(1)}, u32[]{:S(2)}, u32[]{:S(2)}) async-start(bf16[128,4,128]{0,2,1:T(8,128)(2,1)} %bitcast.15), calls=%async_computation.2 | async-start | bytes 262144 | tf_op jit(solution)/shard_map/all_to_all | solution.py:118
  33.4 11.8 %all-to-all-start.3 = ((bf16[128,4,128]{0,2,1:T(8,128)(2,1)}), bf16[128,4,128]{0,2,1:T(8,128)(2,1)S(1)}, u32[]{:S(2)}, u32[]{:S(2)}) async-start(bf16[128,4,128]{0,2,1:T(8,128)(2,1)} %broadcast_select_fusion.4), calls=%async_computation.3 | async-start | bytes 262144 | tf_op jit(solution)/shard_map/all_to_all | solution.py:120
  36.8 0.7 copy-start.4
  36.8 0.7 copy-start.6
  45.2 11.0 %all-to-all-start.4 = ((bf16[128,4,128]{0,2,1:T(8,128)(2,1)}), bf16[128,4,128]{0,2,1:T(8,128)(2,1)S(1)}, u32[]{:S(2)}, u32[]{:S(2)}) async-start(bf16[128,4,128]{0,2,1:T(8,128)(2,1)} %bitcast.24), calls=%async_computation.4 | async-start | bytes 262144 | tf_op jit(solution)/shard_map/all_to_all | solution.py:119
  82.1 9.2 %all-to-all-start.7 = ((bf16[4,2,8192]{2,1,0:T(2,128)(2,1)}), bf16[4,2,8192]{2,1,0:T(2,128)(2,1)S(1)}, u32[]{:S(2)}, u32[]{:S(2)}) async-start(bf16[4,2,8192]{2,1,0:T(2,128)(2,1)} %reshape.270), calls=%async_computation.7 | async-start | bytes 262144 | tf_op jit(solution)/shard_map/all_to_all | solution.py:147
  91.3 9.3 %all-to-all-start.6 = ((bf16[4,2,8192]{2,1,0:T(2,128)(2,1)}), bf16[4,2,8192]{2,1,0:T(2,128)(2,1)S(1)}, u32[]{:S(2)}, u32[]{:S(2)}) async-start(bf16[4,2,8192]{2,1,0:T(2,128)(2,1)} %reshape.268), calls=%async_computation.6 | async-start | bytes 262144 | tf_op jit(solution)/shard_map/all_to_all | solution.py:144
  100.6 18.3 %all-to-all-start.5 = ((bf16[4,2,8192]{2,1,0:T(2,128)(2,1)}), bf16[4,2,8192]{2,1,0:T(2,128)(2,1)S(1)}, u32[]{:S(2)}, u32[]{:S(2)}) async-start(bf16[4,2,8192]{2,1,0:T(2,128)(2,1)} %reshape.266), calls=%async_computation.5 | async-start | bytes 262144 | tf_op jit(solution)/shard_map/all_to_all | solution.py:141
where the time goes:
time: 121 us; the launch traced here: 120 us
  starting transfers between devices  32.2 us (27%)
  waiting for transfers between devices  28.2 us (23%)
  other arithmetic  19.7 us (16%)
  local copies, waits for them, and re-layouts  18.3 us (15%)
  blocking collectives  12.3 us (10%)
  matrix products  7.08 us (6%)
  between operations  1.57 us (1%)
    psum x1, blocking collectives, on_device(): bias_total = lax.psum(jnp.stack(bias_grads, axis=0), 'dp')  12.3 us
    unnamed x36, local copies, waits for them, and re-layouts  10.5 us
    all_to_all x1, starting transfers between devices, on_device(): lax.all_to_all(split_heads(query[0]), 'seq', split_axis=1, concat_axis=0,...  6.48 us
    all_to_all x1, waiting for transfers between devices, on_device(): lax.all_to_all(split_heads(out_ctx[0]), 'seq', split_axis=1, concat_axis=...  5.77 us
    and x8, other arithmetic, slot_scores(): allowed = (slot_at < count_row)[:, None, None] & key_real[:, None, :]  5.77 us
    all_to_all x1, waiting for transfers between devices, on_device(): lax.all_to_all(split_heads(query[0]), 'seq', split_axis=1, concat_axis=0,...  5.31 us
    all_to_all x1, starting transfers between devices, on_device(): lax.all_to_all(split_heads(out_ctx[0]), 'seq', split_axis=1, concat_axis=...  5.07 us
    all_to_all x1, waiting for transfers between devices, on_device(): lax.all_to_all(split_heads(value[0]), 'seq', split_axis=1, concat_axis=0,...  4.94 us
  transfers between devices with their start and end apart: 8, of which 6 were waited for; matrix products, arithmetic and copies ran while one was open for 13% of the time, Pallas kernels for 0%

commit v1 on v0

--- a/solution.py
+++ b/solution.py
@@ -5,6 +5,28 @@
 from jax.sharding import PartitionSpec as P
 
 MASKED = -1000000000.0
+
+
+def in_blocks(shard, dim, size):
+    before, after = (shard.shape[:dim], shard.shape[dim + 1 :])
+    return jnp.moveaxis(shard.reshape(*before, size, -1, *after), dim, 0)
+
+
+def laid_out(parts, dim):
+    shape = list(parts.shape[1:])
+    shape[dim] *= parts.shape[0]
+    return jnp.moveaxis(parts, 0, dim).reshape(shape)
+
+
+def swapped_with_each(x, axis, split_dim, concat_dim):
+    length, index = (lax.axis_size(axis), lax.axis_index(axis))
+    blocks = in_blocks(x, split_dim, length)
+    outs = [blocks[index]]
+    for hop in range(1, length):
+        sent = blocks[index ^ hop]
+        outs.append(lax.ppermute(sent, axis, [(i, i ^ hop) for i in range(length)]))
+    blocks = jnp.stack(outs)[index ^ jnp.arange(length)]
+    return laid_out(blocks, concat_dim)
 
 
 def head_grads(
@@ -144,9 +166,7 @@
         lax.all_to_all(
             jnp.stack(key_grads, axis=1), "seq", split_axis=0, concat_axis=1, tiled=True
         ),
-        lax.all_to_all(
-            jnp.stack(value_grads, axis=1), "seq", split_axis=0, concat_axis=1, tiled=True
-        ),
+        swapped_with_each(jnp.stack(value_grads, axis=1), "seq", 0, 1),
     )
     bias_total = lax.psum(jnp.stack(bias_grads, axis=0), "dp")
     return (

time: 121 us -> 114 us (0.942)
  waiting for transfers between devices: 28.2 us -> 18.5 us
  starting transfers between devices: 32.2 us -> 34.5 us
    all_to_all x1, waiting for transfers between devices: 4.62 us -> 0.01 us  [on_device(): lax.all_to_all(jnp.stack(key_grads, axis=1), 'seq', split_axis=0, concat_...]
    ppermute x0 -> x3, starting transfers between devices: none -> 4.49 us  [swapped_with_each(): outs.append(lax.ppermute(sent, axis, [(i, i ^ hop) for i in range(length)]))]
    all_to_all x1 -> x0, waiting for transfers between devices: 4.45 us -> none  [on_device(): lax.all_to_all(jnp.stack(value_grads, axis=1), 'seq', split_axis=0, conca...]
    all_to_all x1 -> x0, starting transfers between devices: 3.33 us -> none  [on_device(): lax.all_to_all(jnp.stack(value_grads, axis=1), 'seq', split_axis=0, conca...]
    all_to_all x1, starting transfers between devices: 3.46 us -> 6.48 us  [on_device(): lax.all_to_all(split_heads(key[0]), 'seq', split_axis=1, concat_axis=0, t...]
    all_to_all x1, starting transfers between devices: 6.48 us -> 3.46 us  [on_device(): lax.all_to_all(split_heads(query[0]), 'seq', split_axis=1, concat_axis=0,...]
    all_to_all x1, waiting for transfers between devices: 5.31 us -> 2.48 us  [on_device(): lax.all_to_all(split_heads(query[0]), 'seq', split_axis=1, concat_axis=0,...]
    all_to_all x1, waiting for transfers between devices: 3.11 us -> 5.31 us  [on_device(): lax.all_to_all(split_heads(key[0]), 'seq', split_axis=1, concat_axis=0, t...]
  transfers between devices with their start and end apart: 8 -> 10, of which waited for: 6 -> 4; matrix products, arithmetic and copies ran while one was open for 13% -> 13% of each run, Pallas kernels for 0% -> 0%
where the time goes in v1:
time: 114 us; the launch traced here: 112 us
  starting transfers between devices  34.5 us (30%)
  other arithmetic  19.1 us (17%)
  local copies, waits for them, and re-layouts  18.7 us (16%)
  waiting for transfers between devices  18.5 us (16%)
  blocking collectives  12.3 us (11%)
  matrix products  7.06 us (6%)
  between operations  1.57 us (1%)
    psum x1, blocking collectives, on_device(): bias_total = lax.psum(jnp.stack(bias_grads, axis=0), 'dp')  12.3 us
    unnamed x33, local copies, waits for them, and re-layouts  10.3 us
    all_to_all x1, starting transfers between devices, on_device(): lax.all_to_all(split_heads(key[0]), 'seq', split_axis=1, concat_axis=0, t...  6.48 us
    all_to_all x1, waiting for transfers between devices, on_device(): lax.all_to_all(split_heads(out_ctx[0]), 'seq', split_axis=1, concat_axis=...  5.77 us
    and x8, other arithmetic, slot_scores(): allowed = (slot_at < count_row)[:, None, None] & key_real[:, None, :]  5.77 us
    all_to_all x1, waiting for transfers between devices, on_device(): lax.all_to_all(split_heads(key[0]), 'seq', split_axis=1, concat_axis=0, t...  5.31 us
    all_to_all x1, starting transfers between devices, on_device(): lax.all_to_all(split_heads(out_ctx[0]), 'seq', split_axis=1, concat_axis=...  5.07 us
    all_to_all x1, starting transfers between devices, on_device(): lax.all_to_all(jnp.stack(key_grads, axis=1), 'seq', split_axis=0, concat_...  5.01 us
  transfers between devices with their start and end apart: 10, of which 4 were waited for; matrix products, arithmetic and copies ran while one was open for 13% of the time, Pallas kernels for 0%

profile of v1, /device:TPU:0, one launch (start us, length us, event | category | flops | bytes accessed | tf_op | source)
XLA Modules:
  0.0 112.4 jit_solution(13548269285631254748)
XLA Ops:
  0.6 1.7 %copy.93 = bf16[1,128,512]{1,2,0:T(8,128)(2,1)} copy(bf16[1,128,512]{2,1,0:T(8,128)(2,1)} %param.16) | data formatting | bytes 262144 | tf_op args[1]
  2.3 6.5 %all-to-all-start = ((bf16[128,4,128]{0,2,1:T(8,128)(2,1)}), bf16[128,4,128]{0,2,1:T(8,128)(2,1)S(1)}, u32[]{:S(2)}, u32[]{:S(2)}) async-start(bf16[128,4,128]{0,2,1:T(8,128)(2,1)} %bitcast.3), calls=%async_computation | async-start | bytes 262144 | tf_op jit(solution)/shard_map/all_to_all | solution.py:139
  8.8 0.8 copy.94
  9.5 5.3 %all-to-all-done = bf16[128,4,128]{0,2,1:T(8,128)(2,1)S(1)} async-done(((bf16[128,4,128]{0,2,1:T(8,128)(2,1)}), bf16[128,4,128]{0,2,1:T(8,128)(2,1)S(1)}, u32[]{:S(2)}, u32[]{:S(2)}) %all-to-all-start) | async-done | bytes 131104 | tf_op jit(solution)/shard_map/all_to_all | solution.py:139
  14.9 3.5 %all-to-all-start.1 = ((bf16[128,4,128]{0,2,1:T(8,128)(2,1)}), bf16[128,4,128]{0,2,1:T(8,128)(2,1)S(1)}, u32[]{:S(2)}, u32[]{:S(2)}) async-start(bf16[128,4,128]{0,2,1:T(8,128)(2,1)} %bitcast.7), calls=%async_computation.1 | async-start | bytes 262144 | tf_op jit(solution)/shard_map/all_to_all | solution.py:138
  18.4 0.7 copy-done.5
  19.2 0.8 copy.98
  21.0 0.8 copy.100
  21.7 2.5 %all-to-all-done.1 = bf16[128,4,128]{0,2,1:T(8,128)(2,1)S(1)} async-done(((bf16[128,4,128]{0,2,1:T(8,128)(2,1)}), bf16[128,4,128]{0,2,1:T(8,128)(2,1)S(1)}, u32[]{:S(2)}, u32[]{:S(2)}) %all-to-all-start.1) | async-done | bytes 131104 | tf_op jit(solution)/shard_map/all_to_all | solution.py:138
  24.2 3.3 %all-to-all-start.2 = ((bf16[128,4,128]{0,2,1:T(8,128)(2,1)}), bf16[128,4,128]{0,2,1:T(8,128)(2,1)S(1)}, u32[]{:S(2)}, u32[]{:S(2)}) async-start(bf16[128,4,128]{0,2,1:T(8,128)(2,1)} %bitcast.15), calls=%async_computation.2 | async-start | bytes 262144 | tf_op jit(solution)/shard_map/all_to_all | solution.py:140
  27.5 0.7 broadcast_select_fusion.4
  28.5 4.9 %all-to-all-done.2 = bf16[128,4,128]{0,2,1:T(8,128)(2,1)S(1)} async-done(((bf16[128,4,128]{0,2,1:T(8,128)(2,1)}), bf16[128,4,128]{0,2,1:T(8,128)(2,1)S(1)}, u32[]{:S(2)}, u32[]{:S(2)}) %all-to-all-start.2) | async-done | bytes 131104 | tf_op jit(solution)/shard_map/all_to_all | solution.py:140
  33.4 3.3 %all-to-all-start.3 = ((bf16[128,4,128]{0,2,1:T(8,128)(2,1)}), bf16[128,4,128]{0,2,1:T(8,128)(2,1)S(1)}, u32[]{:S(2)}, u32[]{:S(2)}) async-start(bf16[128,4,128]{0,2,1:T(8,128)(2,1)} %broadcast_select_fusion.4), calls=%async_computation.3 | async-start | bytes 262144 | tf_op jit(solution)/shard_map/all_to_all | solution.py:142
  36.8 0.6 copy-done.4
  37.4 7.7 %while.38 = (s32[]{:T(128)}, f32[4,128]{1,0:T(4,128)S(1)}, f32[4,128]{1,0:T(4,128)S(1)}, s32[4]{0:T(128)S(1)}, s32[4,4]{0,1:T(4,128)S(1)}, /*index=5*/s32[]{:T(1...) while((s32[]{:T(128)}, f32[4,128]{1,0:T(4,128)S(1)}, ...), condition=%wide.region_4.6_spmd.clone, body=%wide.region_0.5_spmd.clone.sunk | while | flops 17241176 | bytes 1081720 | solution.py:82
  37.6 0.6 gather_fusion
  38.2 0.7 fusion.84
  39.6 0.6 gather_fusion
  40.2 0.7 fusion.84
  41.5 0.6 gather_fusion
  42.1 0.7 fusion.84
  43.4 0.6 gather_fusion
  44.0 0.7 fusion.84
  45.3 5.1 %all-to-all-start.4 = ((bf16[128,4,128]{0,2,1:T(8,128)(2,1)}), bf16[128,4,128]{0,2,1:T(8,128)(2,1)S(1)}, u32[]{:S(2)}, u32[]{:S(2)}) async-start(bf16[128,4,128]{0,2,1:T(8,128)(2,1)} %bitcast.24), calls=%async_computation.4 | async-start | bytes 262144 | tf_op jit(solution)/shard_map/all_to_all | solution.py:141
  50.5 5.8 %all-to-all-done.4 = bf16[128,4,128]{0,2,1:T(8,128)(2,1)S(1)} async-done(((bf16[128,4,128]{0,2,1:T(8,128)(2,1)}), bf16[128,4,128]{0,2,1:T(8,128)(2,1)S(1)}, u32[]{:S(2)}, u32[]{:S(2)}) %all-to-all-start.4) | async-done | bytes 131104 | tf_op jit(solution)/shard_map/all_to_all | solution.py:141
  56.4 23.8 %while.39 = (s32[]{:T(128)}, f32[4,128,128]{2,1,0:T(8,128)S(1)}, f32[4,128,128]{2,1,0:T(8,128)S(1)}, f32[4,128,128]{2,1,0:T(8,128)S(1)}, f32[4]{0:T(128)S(1)}, /...) while((s32[]{:T(128)}, f32[4,128,128]{2,1,0:T(8,128)S(1)}, ...), condition=%wide.region_12.14_spmd.clone.clone.clone, body=%wide.region_6.0_spmd.clone.clone.clone.sunk | while | flops 85068952 | bytes 5253752 | solution.py:113
  56.6 0.7 fusion.96
  57.3 0.7 fusion.97
  58.0 0.6 gather_fusion.1
  58.6 0.5 fusion.98
  59.2 0.6 gather_fusion.2
  60.6 0.8 scatter_fusion
  61.5 0.8 scatter_fusion.1
  62.6 0.7 fusion.96
  63.3 0.7 fusion.97
  64.0 0.6 gather_fusion.1
  65.1 0.6 gather_fusion.2
  66.5 0.8 scatter_fusion
  67.4 0.8 scatter_fusion.1
  68.5 0.7 fusion.96
  69.3 0.7 fusion.97
  69.9 0.6 gather_fusion.1
  71.1 0.6 gather_fusion.2
  72.5 0.7 scatter_fusion
  73.4 0.7 scatter_fusion.1
  74.5 0.7 fusion.96
  75.2 0.7 fusion.97
  75.9 0.6 gather_fusion.1
  77.0 0.6 gather_fusion.2
  78.4 0.7 scatter_fusion
  79.3 0.7 scatter_fusion.1
  80.8 0.7 reduce.2
  81.5 0.7 reshape.285
  82.1 3.3 %all-to-all-start.5 = ((bf16[4,2,8192]{2,1,0:T(2,128)(2,1)}), bf16[4,2,8192]{2,1,0:T(2,128)(2,1)S(1)}, u32[]{:S(2)}, u32[]{:S(2)}) async-start(bf16[4,2,8192]{2,1,0:T(2,128)(2,1)} %reshape.285), calls=%async_computation.5 | async-start | bytes 262144 | tf_op jit(solution)/shard_map/all_to_all | solution.py:163
  85.5 0.7 reduce.3
  86.2 0.7 reshape.287
  86.9 3.8 %collective-permute-start.2 = (bf16[128,1,128]{2,0,1:T(8,128)(2,1)S(1)}, bf16[128,1,128]{2,0,1:T(8,128)(2,1)S(1)}, u32[]{:S(2)}, u32[]{:S(2)}) collective-permute-start(bf16[128,1,128]{2,0,1:T(8,128)(2,1)S(1)} %get-tuple-element.870), channel_id=1, source_target_pairs={{0,3},{1,2},{2,1},{3,0},{4,7},{5,6},{6,5},{7,4},{8,11},{9,10},{10,... | collective-permute-start | bytes 98312 | tf_op jit(solution)/shard_map/ppermute | solution.py:27
  90.8 0.6 collective-permute-start
  91.4 5.0 %all-to-all-start.6 = ((bf16[4,2,8192]{2,1,0:T(2,128)(2,1)}), bf16[4,2,8192]{2,1,0:T(2,128)(2,1)S(1)}, u32[]{:S(2)}, u32[]{:S(2)}) async-start(bf16[4,2,8192]{2,1,0:T(2,128)(2,1)} %reshape.287), calls=%async_computation.6 | async-start | bytes 262144 | tf_op jit(solution)/shard_map/all_to_all | solution.py:166
  96.4 12.3 %psum.7 = f32[1,4]{1,0:T(1,128)} all-reduce(f32[1,4]{1,0:T(1,128)S(1)} %bitcast.160), channel_id=1, replica_groups=mesh['dp'=8,'seq'=4] {'dp'}, use_global_device_ids=true, to_apply=%region_13.15 | all-reduce | flops 4 | bytes 32 | tf_op jit(solution)/shard_map/psum | solution.py:171
  108.8 0.6 gather_fusion.3
  109.5 0.8 copy.113
  110.6 0.8 copy.111
  111.7 0.8 copy.112
  (143 shorter events, 11.5 us)
Async XLA Ops:
  2.3 6.5 %copy-start = (bf16[1,128,512]{2,1,0:T(8,128)(2,1)S(1)}, bf16[1,128,512]{2,1,0:T(8,128)(2,1)}, u32[]{:S(2)}) copy-start(bf16[1,128,512]{2,1,0:T(8,128)(2,1)} %param.15) | copy-start | bytes 393220
  2.3 12.6 %all-to-all-start = ((bf16[128,4,128]{0,2,1:T(8,128)(2,1)}), bf16[128,4,128]{0,2,1:T(8,128)(2,1)S(1)}, u32[]{:S(2)}, u32[]{:S(2)}) async-start(bf16[128,4,128]{0,2,1:T(8,128)(2,1)} %bitcast.3), calls=%async_computation | async-start | bytes 262144 | tf_op jit(solution)/shard_map/all_to_all | solution.py:139
  14.8 4.3 %copy-start.1 = (bf16[1,128,512]{2,1,0:T(8,128)(2,1)S(1)}, bf16[1,128,512]{2,1,0:T(8,128)(2,1)}, u32[]{:S(2)}) copy-start(bf16[1,128,512]{2,1,0:T(8,128)(2,1)} %param.17) | copy-start | bytes 393220
  14.9 9.4 %all-to-all-start.1 = ((bf16[128,4,128]{0,2,1:T(8,128)(2,1)}), bf16[128,4,128]{0,2,1:T(8,128)(2,1)S(1)}, u32[]{:S(2)}, u32[]{:S(2)}) async-start(bf16[128,4,128]{0,2,1:T(8,128)(2,1)} %bitcast.7), calls=%async_computation.1 | async-start | bytes 262144 | tf_op jit(solution)/shard_map/all_to_all | solution.py:138
  18.4 0.7 copy-start.5
  19.2 0.9 copy-start.2
  20.1 0.9 copy-start.3
  24.2 9.2 %all-to-all-start.2 = ((bf16[128,4,128]{0,2,1:T(8,128)(2,1)}), bf16[128,4,128]{0,2,1:T(8,128)(2,1)S(1)}, u32[]{:S(2)}, u32[]{:S(2)}) async-start(bf16[128,4,128]{0,2,1:T(8,128)(2,1)} %bitcast.15), calls=%async_computation.2 | async-start | bytes 262144 | tf_op jit(solution)/shard_map/all_to_all | solution.py:140
  33.4 11.9 %all-to-all-start.3 = ((bf16[128,4,128]{0,2,1:T(8,128)(2,1)}), bf16[128,4,128]{0,2,1:T(8,128)(2,1)S(1)}, u32[]{:S(2)}, u32[]{:S(2)}) async-start(bf16[128,4,128]{0,2,1:T(8,128)(2,1)} %broadcast_select_fusion.4), calls=%async_computation.3 | async-start | bytes 262144 | tf_op jit(solution)/shard_map/all_to_all | solution.py:142
  36.8 0.7 copy-start.4
  36.8 0.7 copy-start.6
  45.3 11.0 %all-to-all-start.4 = ((bf16[128,4,128]{0,2,1:T(8,128)(2,1)}), bf16[128,4,128]{0,2,1:T(8,128)(2,1)S(1)}, u32[]{:S(2)}, u32[]{:S(2)}) async-start(bf16[128,4,128]{0,2,1:T(8,128)(2,1)} %bitcast.24), calls=%async_computation.4 | async-start | bytes 262144 | tf_op jit(solution)/shard_map/all_to_all | solution.py:141
  82.1 9.3 %all-to-all-start.5 = ((bf16[4,2,8192]{2,1,0:T(2,128)(2,1)}), bf16[4,2,8192]{2,1,0:T(2,128)(2,1)S(1)}, u32[]{:S(2)}, u32[]{:S(2)}) async-start(bf16[4,2,8192]{2,1,0:T(2,128)(2,1)} %reshape.285), calls=%async_computation.5 | async-start | bytes 262144 | tf_op jit(solution)/shard_map/all_to_all | solution.py:163
  86.9 21.9 %collective-permute-start.2 = (bf16[128,1,128]{2,0,1:T(8,128)(2,1)S(1)}, bf16[128,1,128]{2,0,1:T(8,128)(2,1)S(1)}, u32[]{:S(2)}, u32[]{:S(2)}) collective-permute-start(bf16[128,1,128]{2,0,1:T(8,128)(2,1)S(1)} %get-tuple-element.870), channel_id=1, source_target_pairs={{0,3},{1,2},{2,1},{3,0},{4,7},{5,6},{6,5},{7,4},{8,11},{9,10},{10,... | collective-permute-start | bytes 98312 | tf_op jit(solution)/shard_map/ppermute | solution.py:27
  90.8 18.0 %collective-permute-start.1 = (bf16[128,1,128]{2,0,1:T(8,128)(2,1)S(1)}, bf16[128,1,128]{2,0,1:T(8,128)(2,1)S(1)}, u32[]{:S(2)}, u32[]{:S(2)}) collective-permute-start(bf16[128,1,128]{2,0,1:T(8,128)(2,1)S(1)} %get-tuple-element.871), channel_id=1, source_target_pairs={{0,2},{1,3},{2,0},{3,1},{4,6},{5,7},{6,4},{7,5},{8,10},{9,11},{10,... | collective-permute-start | bytes 98312 | tf_op jit(solution)/shard_map/ppermute | solution.py:27
  90.8 18.0 %collective-permute-start = (bf16[128,1,128]{2,0,1:T(8,128)(2,1)S(1)}, bf16[128,1,128]{2,0,1:T(8,128)(2,1)S(1)}, u32[]{:S(2)}, u32[]{:S(2)}) collective-permute-start(bf16[128,1,128]{2,0,1:T(8,128)(2,1)S(1)} %get-tuple-element.872), channel_id=1, source_target_pairs={{0,1},{1,0},{2,3},{3,2},{4,5},{5,4},{6,7},{7,6},{8,9},{9,8},{10,11... | collective-permute-start | bytes 98312 | tf_op jit(solution)/shard_map/ppermute | solution.py:27
  91.4 20.0 %all-to-all-start.6 = ((bf16[4,2,8192]{2,1,0:T(2,128)(2,1)}), bf16[4,2,8192]{2,1,0:T(2,128)(2,1)S(1)}, u32[]{:S(2)}, u32[]{:S(2)}) async-start(bf16[4,2,8192]{2,1,0:T(2,128)(2,1)} %reshape.287), calls=%async_computation.6 | async-start | bytes 262144 | tf_op jit(solution)/shard_map/all_to_all | solution.py:166
